TPU v7x, 32 devices: a whole 2x2x4 slice. The times are simulated.
32 devices in a mesh: dp: 8 (over z, y), rep: 4 (over x, core).
Axes of the slice: x: 2, y: 2, z: 4, core: 2. Of those that a mesh axis runs over, the one named last changes fastest.
Arguments:
- block_in: bfloat16 [4, 12288, 2048], P('rep', 'dp')
- crop_codes: int32 [4, 1, 96], P('rep'), may hold values from 0 to 4, as said below
- tile_perm: int32 [4, 1, 768], P('rep'), may hold values from 0 to 767, each once within a row
- reduce_weight: bfloat16 [2048, 512], replicated, may hold values from -0.125 to 0.125
- dilated_weight: bfloat16 [4608, 512], replicated, may hold values from -0.09375 to 0.09375
- expand_weight: bfloat16 [512, 2048], replicated, may hold values from -0.25 to 0.25
- first_gain: float32 [512], replicated, may hold values from 0.5 to 1.5
- first_bias: float32 [512], replicated, may hold values from -1.5 to 1.5
- middle_gain: float32 [512], replicated, may hold values from 0.5 to 1.5
- middle_bias: float32 [512], replicated, may hold values from -1.5 to 1.5
- last_gain: float32 [2048], replicated, may hold values from 0.5 to 1.5
- last_bias: float32 [2048], replicated, may hold values from -1.5 to 1.5
- cotangent: bfloat16 [4, 12288, 2048], P('rep', 'dp'), may hold values from -6 to 6
Outputs:
- block_out: bfloat16 [4, 12288, 2048], P('rep', 'dp')
- grad_in: float32 [4, 12288, 2048], P('rep', 'dp')
- reduce_grad: float32 [2048, 512], replicated
- dilated_grad: float32 [4608, 512], replicated
- expand_grad: float32 [512, 2048], replicated
- first_gain_grad: float32 [512], replicated
- first_bias_grad: float32 [512], replicated
- middle_gain_grad: float32 [512], replicated
- middle_bias_grad: float32 [512], replicated
- last_gain_grad: float32 [2048], replicated
- final_bias_gradient: float32 [2048], replicated
Inputs may be any that keep to these rules, and one draw needn't show every extreme that they name: `crop_codes`: in every group and set the first slot is 4, the tile counts 8 u u of the slots sum to exactly 768, and the slots after the last crop are 0. tile_perm[r, s] is a permutation.
All inputs are finite; a program needn't handle non-finite values.
Results may differ from a plain program's by a relative error of at most 0.012.
Values may be sent and summed in bfloat16 or wider, within the bound.
No kernel may reach another device: no remote copies, remote signals or barrier semaphores. Data moves between devices by JAX's collectives and lax.ppermute only.
A program may use at most 256 MiB of HBM per device.

v0:
```python
import jax
import jax.numpy as jnp
from jax import lax
from jax.sharding import PartitionSpec as P

EPS = 1e-05


def crop_tables(codes, tiles):
    slots = codes.shape[0]
    sizes = 8 * codes * codes
    ending = jnp.cumsum(sizes, dtype=jnp.int32)
    starting = ending - sizes
    number = jnp.arange(tiles, dtype=jnp.int32)
    owner = jnp.sum((ending[None, :] <= number[:, None]).astype(jnp.int32), axis=1, dtype=jnp.int32)
    onehot = (owner[:, None] == jnp.arange(slots, dtype=jnp.int32)[None, :]).astype(jnp.int32)
    first = jnp.sum(onehot * starting[None, :], axis=1, dtype=jnp.int32)
    scale = jnp.sum(onehot * codes[None, :], axis=1, dtype=jnp.int32)
    width = 4 * scale
    height = 2 * scale
    local = number - first
    across = local // width
    along = local % width
    columns = []
    for shift_row in (-1, 0, 1):
        for shift_col in (-1, 0, 1):
            inside = (
                (across + shift_row >= 0)
                & (across + shift_row < height)
                & (along + shift_col >= 0)
                & (along + shift_col < width)
            )
            columns.append(jnp.where(inside, number + shift_row * width + shift_col, tiles))
    return jnp.stack(columns, axis=1)


def silu_slope(values):
    sig = jax.nn.sigmoid(values)
    return sig * (1.0 + values * (1.0 - sig))


def norm_forward(hidden, total_rows):
    sums, squares = lax.psum(
        (jnp.sum(hidden, axis=0), jnp.sum(hidden * hidden, axis=0)), ("dp", "rep")
    )
    mean = sums / total_rows
    scale = lax.rsqrt(squares / total_rows - mean * mean + EPS)
    return ((hidden - mean) * scale, scale)


def norm_backward(upstream, normed, gain, scale, total_rows):
    shift, tilt = lax.psum(
        (jnp.sum(upstream, axis=0), jnp.sum(upstream * normed, axis=0)), ("dp", "rep")
    )
    grad_hidden = gain * scale * (upstream - (shift + normed * tilt) / total_rows)
    return (grad_hidden.astype(jnp.bfloat16), shift, tilt)


def contract_rows(left, right):
    return lax.dot_general(
        left, right, (((0,), (0,)), ((), ())), preferred_element_type=jnp.float32
    )


def contract_cols(left, right):
    return lax.dot_general(
        left, right, (((1,), (1,)), ((), ())), preferred_element_type=jnp.float32
    )


def body(
    block_in,
    crop_codes,
    tile_perm,
    reduce_weight,
    dilated_weight,
    expand_weight,
    first_gain,
    first_bias,
    middle_gain,
    middle_bias,
    last_gain,
    last_bias,
    cotangent,
):
    devices = lax.axis_size("dp")
    replicas = lax.axis_size("rep")
    sets = max(devices // 16, 1)
    phase_dev = 16 * sets // devices
    inputs = block_in[0]
    pixels = inputs.shape[0]
    middle = reduce_weight.shape[1]
    tiles = tile_perm.shape[2]
    per_device = tiles // devices
    total_rows = float(pixels * devices * replicas)
    set_index = lax.axis_index("dp") * phase_dev // 16
    codes = lax.dynamic_index_in_dim(crop_codes[0], set_index, 0, keepdims=False)
    ordering = lax.dynamic_index_in_dim(tile_perm[0], set_index, 0, keepdims=False)
    inverse = jnp.argsort(ordering)
    neighbors = crop_tables(codes, tiles)
    mirrored = neighbors[:, ::-1]
    hidden_one = jnp.dot(inputs, reduce_weight, preferred_element_type=jnp.float32)
    normed_one, scale_one = norm_forward(hidden_one, total_rows)
    pre_one = first_gain * normed_one + first_bias
    act_one = jax.nn.silu(pre_one).astype(jnp.bfloat16)
    arrived = lax.all_to_all(
        act_one.reshape(devices, phase_dev, per_device, middle),
        "dp",
        split_axis=0,
        concat_axis=2,
        tiled=True,
    )
    phase_activation = jnp.take(arrived.reshape(phase_dev, tiles, middle), inverse, axis=1)
    padded = jnp.concatenate(
        [phase_activation, jnp.zeros((phase_dev, 1, middle), jnp.bfloat16)], axis=1
    )
    columns = jnp.take(padded, neighbors, axis=1).reshape(pixels, 9 * middle)
    hidden_two = jnp.dot(columns, dilated_weight, preferred_element_type=jnp.float32)
    normed_two, scale_two = norm_forward(hidden_two, total_rows)
    preactivation_second = middle_gain * normed_two + middle_bias
    act_two = jax.nn.silu(preactivation_second).astype(jnp.bfloat16)
    leaving = jnp.take(act_two.reshape(phase_dev, tiles, middle), ordering, axis=1).reshape(
        phase_dev, devices, per_device, middle
    )
    act_back = lax.all_to_all(leaving, "dp", split_axis=1, concat_axis=0, tiled=True).reshape(
        pixels, middle
    )
    hidden_three = jnp.dot(act_back, expand_weight, preferred_element_type=jnp.float32)
    normed_three, scale_three = norm_forward(hidden_three, total_rows)
    summed = last_gain * normed_three + last_bias + inputs.astype(jnp.float32)
    block_out = jax.nn.silu(summed).astype(jnp.bfloat16)
    grad_sum = cotangent[0].astype(jnp.float32) * silu_slope(summed)
    grad_three, final_bias_gradient, last_gain_grad = norm_backward(
        grad_sum, normed_three, last_gain, scale_three, total_rows
    )
    expand_grad = contract_rows(act_back, grad_three)
    grad_act_two = contract_cols(grad_three, expand_weight).astype(jnp.bfloat16)
    returned_values = lax.all_to_all(
        grad_act_two.reshape(devices, phase_dev, per_device, middle),
        "dp",
        split_axis=0,
        concat_axis=2,
        tiled=True,
    )
    grad_phase = jnp.take(
        returned_values.reshape(phase_dev, tiles, middle), inverse, axis=1
    ).reshape(pixels, middle)
    incoming_gradient_second = grad_phase.astype(jnp.float32) * silu_slope(preactivation_second)
    grad_two, middle_bias_grad, middle_gain_grad = norm_backward(
        incoming_gradient_second, normed_two, middle_gain, scale_two, total_rows
    )
    dilated_grad = contract_rows(columns, grad_two)
    grad_columns = contract_cols(grad_two, dilated_weight).reshape(phase_dev, tiles, 9, middle)
    padded_grad = jnp.concatenate(
        [grad_columns, jnp.zeros((phase_dev, 1, 9, middle), jnp.float32)], axis=1
    )
    grad_act_one = jnp.zeros((phase_dev, tiles, middle), jnp.float32)
    for offset in range(9):
        grad_act_one = grad_act_one + jnp.take(
            padded_grad[:, :, offset, :], mirrored[:, offset], axis=1
        )
    outgoing = jnp.take(grad_act_one.astype(jnp.bfloat16), ordering, axis=1).reshape(
        phase_dev, devices, per_device, middle
    )
    grad_pixels = lax.all_to_all(outgoing, "dp", split_axis=1, concat_axis=0, tiled=True).reshape(
        pixels, middle
    )
    upstream_one = grad_pixels.astype(jnp.float32) * silu_slope(pre_one)
    grad_one, first_bias_grad, first_gain_grad = norm_backward(
        upstream_one, normed_one, first_gain, scale_one, total_rows
    )
    reduce_grad = contract_rows(inputs, grad_one)
    grad_in = contract_cols(grad_one, reduce_weight) + grad_sum
    reduce_grad, dilated_grad, expand_grad = lax.psum(
        (reduce_grad, dilated_grad, expand_grad), ("dp", "rep")
    )
    return (
        block_out[None],
        grad_in[None],
        reduce_grad,
        dilated_grad,
        expand_grad,
        first_gain_grad,
        first_bias_grad,
        middle_gain_grad,
        middle_bias_grad,
        last_gain_grad,
        final_bias_gradient,
    )


def solution(mesh):
    in_specs = (
        P("rep", "dp", None),
        P("rep", None, None),
        P("rep", None, None),
        P(),
        P(),
        P(),
        P(),
        P(),
        P(),
        P(),
        P(),
        P(),
        P("rep", "dp", None),
    )
    out_specs = (
        P("rep", "dp", None),
        P("rep", "dp", None),
        P(),
        P(),
        P(),
        P(),
        P(),
        P(),
        P(),
        P(),
        P(),
    )
    return jax.shard_map(body, mesh=mesh, in_specs=in_specs, out_specs=out_specs, check_vma=False)
```

profile of v0, /device:TPU:0, one launch (start us, length us, event | category | flops | bytes accessed | tf_op | source)
XLA Modules:
  0.0 1226.2 jit_solution(3939753884476722350)
XLA Ops:
  16.0 42.0 %all-reduce.7 = (f32[512]{0:T(512)S(1)}, f32[512]{0:T(512)S(1)}) all-reduce(f32[512]{0:T(512)S(1)} %get-tuple-element.92, f32[512]{0:T(512)S(1)} %get-tuple-element.91), channel_id=1, replica_groups=mesh['dp'=8,'rep'=4] {'dp','rep'}, use_global_device_ids=true, to_apply=%region_7.8 | all-reduce | flops 1024 | bytes 8192 | tf_op jit(solution)/shard_map/psum | solution.py:43
  76.8 27.8 %all-to-all-done = bf16[8,2,96,512]{3,2,1,0:T(8,128)(2,1)} async-done(((bf16[8,2,96,512]{3,2,1,0:T(8,128)(2,1)}), bf16[8,2,96,512]{3,2,1,0:T(8,128)(2,1)}, u32[]{:S(2)}, u32[]{:S(2)}) %all-to-all-start) | async-done | bytes 1572896 | tf_op jit(solution)/shard_map/all_to_all | solution.py:106
  123.4 41.2 %gather_fusion = bf16[6912,2,512]{2,1,0:T(2,128)(2,1)} fusion(bf16[2,769,512]{2,0,1:T(2,128)(2,1)} %concatenate.27, s32[7168]{0:T(1024)S(1)} %pad_clamp_fusion), kind=kCustom, calls=%fused_computation.13 | custom fusion | bytes 28339200 | tf_op jit(solution)/shard_map/jit(_take)/gather | solution.py:117
  164.6 46.0 %copy.157 = bf16[768,9,2,512]{0,2,3,1:T(2,128)(2,1)} copy(bf16[768,9,2,512]{3,2,1,0:T(2,128)(2,1)} %bitcast.171) | data formatting | bytes 28311552 | tf_op jit(solution)/shard_map/jit(_take)/gather | solution.py:117
  210.6 14.0 %broadcast_select_fusion = bf16[768,9,2,512]{0,2,3,1:T(2,128)(2,1)S(1)} fusion(bf16[768,9,2,512]{0,2,3,1:T(2,128)(2,1)} %copy.157, pred[768,9]{0,1:T(8,128)(4,1)S(1)} %compare_and_fusion), kind=kLoop, calls=%fused_computation.14 | loop fusion | flops 7077888 | bytes 28318464 | tf_op jit(solution)/shard_map/jit(_take)/select_n | solution.py:117
  231.9 13.0 %fusion.20 = (f32[512]{0:T(512)S(1)}, f32[512]{0:T(512)S(1)}, f32[1536,512]{1,0:T(8,128)}) fusion(bf16[1536,4608]{0,1:T(8,128)(2,1)S(1)} %bitcast.173, bf16[4608,512]{1,0:T(8,128)(2,1)} %param.21), kind=kOutput, calls=%fused_computation.183 | convolution fusion | flops 7250115584 | bytes 22024192 | tf_op jit(solution)/shard_map/dot_general | solution.py:118
  244.9 37.5 %all-reduce.6 = (f32[512]{0:T(512)S(1)}, f32[512]{0:T(512)S(1)}) all-reduce(f32[512]{0:T(512)S(1)} %get-tuple-element.90, f32[512]{0:T(512)S(1)} %get-tuple-element.89), channel_id=1, replica_groups=mesh['dp'=8,'rep'=4] {'dp','rep'}, use_global_device_ids=true, to_apply=%region_12.14 | all-reduce | flops 1024 | bytes 8192 | tf_op jit(solution)/shard_map/psum | solution.py:43
  300.5 41.2 %all_to_all.54 = bf16[2,8,96,512]{3,2,0,1:T(8,128)(2,1)S(1)} all-to-all(bf16[2,8,96,512]{3,2,0,1:T(8,128)(2,1)S(1)} %copy.159), channel_id=1, replica_groups=mesh['dp'=8,'rep'=4] {'dp'}, dimensions={1} | all-to-all | bytes 3145728 | tf_op jit(solution)/shard_map/all_to_all | solution.py:125
  348.4 39.4 %all-reduce.5 = (f32[2048]{0:T(1024)S(1)}, f32[2048]{0:T(1024)S(1)}) all-reduce(f32[2048]{0:T(1024)S(1)} %get-tuple-element.84, f32[2048]{0:T(1024)S(1)} %get-tuple-element.83), channel_id=1, replica_groups=mesh['dp'=8,'rep'=4] {'dp','rep'}, use_global_device_ids=true, to_apply=%region_16.18 | all-reduce | flops 4096 | bytes 32768 | tf_op jit(solution)/shard_map/psum | solution.py:43
  387.8 19.9 %fusion.17 = (f32[2048]{0:T(1024)S(1)}, f32[2048]{0:T(1024)S(1)}, f32[1536,2048]{1,0:T(8,128)}, bf16[1,1536,2048]{2,1,0:T(8,128)(2,1)}) fusion(f32[2048]{0:T(1024)S(1)} %get-tuple-element.169, f32[1536,2048]{1,0:T(8,128)} %get-tuple-element.203, f32[2048]{0:T(1024)S(1)} %get-tuple-element.186, bf16[1,1536,2048]{2,1,0:T(8,128)(2,1)} %param.17, ...), kind=kLoop, calls=%fused_computation.180 | loop fusion | flops 62910464 | bytes 44089344 | tf_op jit(solution)/shard_map/reduce_sum | solution.py:53
  407.7 40.5 %all-reduce.4 = (f32[2048]{0:T(1024)S(1)}, f32[2048]{0:T(1024)S(1)}) all-reduce(f32[2048]{0:T(1024)S(1)} %get-tuple-element.82, f32[2048]{0:T(1024)S(1)} %get-tuple-element.81), channel_id=1, replica_groups=mesh['dp'=8,'rep'=4] {'dp','rep'}, use_global_device_ids=true, to_apply=%region_20.22 | all-reduce | flops 4096 | bytes 32768 | tf_op jit(solution)/shard_map/psum | solution.py:52
  448.2 9.6 multiply_convert_fusion
  467.6 35.8 %all-to-all-done.2 = bf16[8,2,96,512]{3,2,1,0:T(8,128)(2,1)S(1)} async-done(((bf16[8,2,96,512]{3,2,1,0:T(8,128)(2,1)}), bf16[8,2,96,512]{3,2,1,0:T(8,128)(2,1)S(1)}, u32[]{:S(2)}, u32[]{:S(2)}) %all-to-all-start.2) | async-done | bytes 1572896 | tf_op jit(solution)/shard_map/all_to_all | solution.py:138
  514.9 37.8 %all-reduce.3 = (f32[512]{0:T(512)S(1)}, f32[512]{0:T(512)S(1)}) all-reduce(f32[512]{0:T(512)S(1)} %get-tuple-element.86, f32[512]{0:T(512)S(1)} %get-tuple-element.85), channel_id=1, replica_groups=mesh['dp'=8,'rep'=4] {'dp','rep'}, use_global_device_ids=true, to_apply=%region_24.26 | all-reduce | flops 1024 | bytes 8192 | tf_op jit(solution)/shard_map/psum | solution.py:52
  557.3 15.2 %fusion.23 = f32[1536,4608]{0,1:T(8,128)} fusion(bf16[1536,512]{1,0:T(8,128)(2,1)S(1)} %multiply_convert_fusion.3, bf16[4608,512]{1,0:T(8,128)(2,1)} %param.21), kind=kOutput, calls=%fused_computation.185 | convolution fusion | flops 7247757312 | bytes 34603008 | tf_op jit(solution)/shard_map/dot_general | solution.py:66
  572.5 33.0 %reshape.981 = f32[2,768,9,512]{1,0,3,2:T(2,128)} reshape(f32[1536,4608]{0,1:T(8,128)} %fusion.23) | data formatting | bytes 56623104 | tf_op jit(solution)/shard_map/reshape | solution.py:153
  605.4 21.1 %slice_bitcast_fusion.8 = (f32[2,769,512]{1,0,2:T(2,128)}, f32[2,769,512]{1,0,2:T(2,128)}, f32[2,769,512]{1,0,2:T(2,128)}, f32[2,769,512]{1,0,2:T(2,128)}, f32[2...) fusion(f32[2,768,9,512]{1,0,3,2:T(2,128)} %reshape.981), kind=kLoop, calls=%fused_computation.37 | loop fusion | bytes 56659968 | tf_op jit(solution)/shard_map/squeeze | solution.py:160
  751.2 9.3 gather_fusion.9
  787.3 16.0 %fusion.8 = bf16[2,768,512]{2,0,1:T(2,128)(2,1)S(1)} fusion(f32[768,2,512]{2,1,0:T(2,128)} %gather_fusion.12, f32[768,2,512]{2,1,0:T(2,128)} %gather_fusion.11, f32[768,2,512]{2,1,0:T(2,128)} %gather_fusion.10, f32[768,2,512]{2,1,0:T(2,128)} %gather_fusion.9, f32[768,2,512]{2,1,0:T(2,128)} %gather_fusion.8, f32[768,2,512]{2,1,0:T(2,128)} %gather_fusion.7, ...), kind=kLoop, calls=%fused_computation.42 | loop fusion | flops 14155776 | bytes 29891328 | tf_op jit(solution)/shard_map/convert_element_type | solution.py:162
  829.1 12.9 %fusion.24 = f32[4608,512]{1,0:T(8,128)} fusion(bf16[1536,4608]{0,1:T(8,128)(2,1)} %bitcast.174, bf16[1536,512]{1,0:T(8,128)(2,1)S(1)} %copy-done.9), kind=kOutput, calls=%fused_computation.186 | convolution fusion | flops 7247757312 | bytes 25165824 | tf_op jit(solution)/shard_map/dot_general | solution.py:60
  842.1 13.7 %all-to-all-done.3 = bf16[2,8,96,512]{3,2,0,1:T(8,128)(2,1)S(1)} async-done(((bf16[2,8,96,512]{3,2,0,1:T(8,128)(2,1)}), bf16[2,8,96,512]{3,2,0,1:T(8,128)(2,1)S(1)}, u32[]{:S(2)}, u32[]{:S(2)}) %all-to-all-start.3) | async-done | bytes 1572896 | tf_op jit(solution)/shard_map/all_to_all | solution.py:165
  861.0 37.6 %all-reduce.2 = (f32[512]{0:T(512)S(1)}, f32[512]{0:T(512)S(1)}) all-reduce(f32[512]{0:T(512)S(1)} %get-tuple-element.88, f32[512]{0:T(512)S(1)} %get-tuple-element.87), channel_id=1, replica_groups=mesh['dp'=8,'rep'=4] {'dp','rep'}, use_global_device_ids=true, to_apply=%region_28.31 | all-reduce | flops 1024 | bytes 8192 | tf_op jit(solution)/shard_map/psum | solution.py:52
  910.1 10.5 add_bitcast_fusion
  920.6 282.4 %all-reduce.11.cloned.1.call-done = (f32[2048,512]{0,1:T(8,128)}, f32[4608,512]{1,0:T(8,128)}, f32[512,2048]{1,0:T(8,128)}) async-done(((f32[2048,512]{0,1:T(8,128)}, f32[4608,512]{1,0:T(8,128)}, f32[512,2048]{1,0:T(8,128)}), (f32[2048,512]{0,1:T(8,128)}, f32[4608,512]{1,0:T(8,128)}, f32[512,2048]{1,0:T(8,128)})) %all-reduce.11.cloned.1.call-update) | async-done | bytes 17825808 | tf_op jit(solution)/shard_map/psum | solution.py:174
  (163 shorter events, 314.2 us)
Async XLA Ops:
  7.2 334.6 %copy-start = (bf16[512,2048]{1,0:T(8,128)(2,1)S(1)}, bf16[512,2048]{1,0:T(8,128)(2,1)}, u32[]{:S(2)}) copy-start(bf16[512,2048]{1,0:T(8,128)(2,1)} %param.22) | copy-start | bytes 6291460
  7.2 50.7 %copy-start.17 = (f32[512]{0:T(512)S(1)}, f32[512]{0:T(512)}, u32[]{:S(2)}) copy-start(f32[512]{0:T(512)} %param.23) | copy-start | bytes 6148
  7.2 51.9 %copy-start.23 = (f32[512]{0:T(512)S(1)}, f32[512]{0:T(512)}, u32[]{:S(2)}) copy-start(f32[512]{0:T(512)} %param.24) | copy-start | bytes 6148
  59.1 9.9 copy-start.32
  59.1 10.4 copy-start.27
  63.1 41.5 %all-to-all-start = ((bf16[8,2,96,512]{3,2,1,0:T(8,128)(2,1)}), bf16[8,2,96,512]{3,2,1,0:T(8,128)(2,1)}, u32[]{:S(2)}, u32[]{:S(2)}) async-start(bf16[8,2,96,512]{3,2,1,0:T(8,128)(2,1)} %bitcast.179), calls=%async_computation | async-start | bytes 3145728 | tf_op jit(solution)/shard_map/all_to_all | solution.py:106
  231.9 13.0 %copy-start.4 = (bf16[576,8,2,768]{3,1,2,0:T(8,128)(2,1)}, bf16[576,8,2,768]{3,1,2,0:T(8,128)(2,1)S(1)}, u32[]{:S(2)}) copy-start(bf16[576,8,2,768]{3,1,2,0:T(8,128)(2,1)S(1)} %copy.206) | copy-start | bytes 42467332
  231.9 50.5 %copy-start.10 = (f32[512]{0:T(512)S(1)}, f32[512]{0:T(512)}, u32[]{:S(2)}) copy-start(f32[512]{0:T(512)} %param.25) | copy-start | bytes 6148
  231.9 50.5 %copy-start.16 = (f32[512]{0:T(512)S(1)}, f32[512]{0:T(512)}, u32[]{:S(2)}) copy-start(f32[512]{0:T(512)} %param.26) | copy-start | bytes 6148
  341.8 46.0 %copy-start.15 = (f32[2048]{0:T(1024)S(1)}, f32[2048]{0:T(1024)}, u32[]{:S(2)}) copy-start(f32[2048]{0:T(1024)} %param.27) | copy-start | bytes 24580
  341.8 46.0 %copy-start.20 = (f32[2048]{0:T(1024)S(1)}, f32[2048]{0:T(1024)}, u32[]{:S(2)}) copy-start(f32[2048]{0:T(1024)} %param.28) | copy-start | bytes 24580
  448.2 9.6 copy-start.21
  448.2 9.6 copy-start.22
  462.7 40.7 %all-to-all-start.2 = ((bf16[8,2,96,512]{3,2,1,0:T(8,128)(2,1)}), bf16[8,2,96,512]{3,2,1,0:T(8,128)(2,1)S(1)}, u32[]{:S(2)}, u32[]{:S(2)}) async-start(bf16[8,2,96,512]{3,2,1,0:T(8,128)(2,1)} %bitcast.183), calls=%async_computation.2 | async-start | bytes 3145728 | tf_op jit(solution)/shard_map/all_to_all | solution.py:138
  778.4 8.9 copy-start.26
  814.3 41.5 %all-to-all-start.3 = ((bf16[2,8,96,512]{3,2,0,1:T(8,128)(2,1)}), bf16[2,8,96,512]{3,2,0,1:T(8,128)(2,1)S(1)}, u32[]{:S(2)}, u32[]{:S(2)}) async-start(bf16[2,8,96,512]{3,2,0,1:T(8,128)(2,1)} %copy.183), calls=%async_computation.3 | async-start | bytes 3145728 | tf_op jit(solution)/shard_map/all_to_all | solution.py:165
  820.2 382.8 %all-reduce.11.cloned.1.call-start = ((), (), s32[]{:S(2)}) async-start(), calls=%async_computation.4 | async-start | bytes 35651584 | tf_op jit(solution)/shard_map/psum | solution.py:174
  820.3 8.9 copy-start.9
  842.1 14.2 %copy-start.12 = (f32[512]{0:T(512)S(1)}, f32[512]{0:T(512)}, u32[]{:S(2)}) copy-start(f32[512]{0:T(512)} %copy-done.11) | copy-start | bytes 6148
  842.1 14.2 %copy-start.14 = (f32[512]{0:T(512)S(1)}, f32[512]{0:T(512)}, u32[]{:S(2)}) copy-start(f32[512]{0:T(512)} %copy-done.13) | copy-start | bytes 6148
  842.1 14.2 %copy-start.18 = (f32[512]{0:T(512)S(1)}, f32[512]{0:T(512)}, u32[]{:S(2)}) copy-start(f32[512]{0:T(512)} %param.23) | copy-start | bytes 6148
  842.1 14.2 %copy-start.24 = (f32[512]{0:T(512)S(1)}, f32[512]{0:T(512)}, u32[]{:S(2)}) copy-start(f32[512]{0:T(512)} %param.24) | copy-start | bytes 6148
  857.7 40.9 %copy-start.25 = (f32[512]{0:T(512)S(1)}, f32[512]{0:T(512)}, u32[]{:S(2)}) copy-start(f32[512]{0:T(512)} %get-tuple-element.187) | copy-start | bytes 6148
  1208.4 10.8 copy-start.1
  (13 other events, 54.0 us)
Sparse Core Ops, SparseCore 0:
  910.3 292.7 all-reduce.10
where the time goes:
time: 1240 us; the launch traced here: 1230 us
  local copies, waits for them, and re-layouts  370 us (30%)
  waiting for transfers between devices  360 us (29%)
  blocking collectives  276 us (22%)
  other arithmetic  101 us (8%)
  matrix products  88.3 us (7%)
  starting transfers between devices  16.4 us (1%)
  between operations  14.8 us (1%)
    psum x1, waiting for transfers between devices, body(): lax.psum((reduce_grad, dilated_grad, expand_grad), ('dp', 'rep'))  282 us
    psum x3, blocking collectives, norm_forward(): lax.psum((jnp.sum(hidden, axis=0), jnp.sum(hidden * hidden, axis=0)), ('d...  119 us
    psum x3, blocking collectives, norm_backward(): lax.psum((jnp.sum(upstream, axis=0), jnp.sum(upstream * normed, axis=0)),...  116 us
    squeeze x10, local copies, waits for them, and re-layouts, body(): padded_grad[:, :, offset, :]  101 us
    gather x2, local copies, waits for them, and re-layouts, body(): columns = jnp.take(padded, neighbors, axis=1).reshape(pixels, 9 * middle)  87.2 us
    gather x9, local copies, waits for them, and re-layouts, body(): jnp.take(padded_grad[:, :, offset, :], mirrored[:, offset], axis=1)  81 us
    all_to_all x1, blocking collectives, body(): lax.all_to_all(leaving, 'dp', split_axis=1, concat_axis=0, tiled=True)  41.2 us
    all_to_all x1, waiting for transfers between devices, body(): lax.all_to_all(grad_act_two.reshape(devices, phase_dev, per_device, middl...  35.8 us
  transfers between devices with their start and end apart: 4, of which 4 were waited for; matrix products, arithmetic and copies ran while one was open for 3% of the time, Pallas kernels for 0%

commit v1 on v0

v1 whole, which is shorter than its diff:
```python
import jax
import jax.numpy as jnp
from jax import lax
from jax.experimental import pallas as pl
from jax.experimental.pallas import tpu as pltpu
from jax.sharding import PartitionSpec as P

EPS = 1e-05
F32 = jnp.float32
BF16 = jnp.bfloat16
VMEM_BYTES = 58 * 1024 * 1024
BLOCKS = 8
AXES = ("dp", "rep")


def params(grid_rank=0):
    kwargs = {"vmem_limit_bytes": VMEM_BYTES}
    if grid_rank:
        kwargs["dimension_semantics"] = ("arbitrary",) * grid_rank
    return pltpu.CompilerParams(**kwargs)


def sigmoid(v):
    return 0.5 * jnp.tanh(0.5 * v) + 0.5


def dot(a, b, dims=((1,), (0,))):
    return lax.dot_general(a, b, (dims, ((), ())), preferred_element_type=F32)


def moments(sums, total):
    mean = sums[0:1] / total
    scale = lax.rsqrt(sums[1:2] / total - mean * mean + EPS)
    return mean, scale


def column_sums(a, b):
    return jnp.concatenate(
        [jnp.sum(a, axis=0, keepdims=True), jnp.sum(b, axis=0, keepdims=True)], axis=0
    )


def xor_blocks(values, me):
    for bit in range(3):
        paired = values.reshape((BLOCKS >> (bit + 1), 2, 1 << bit) + values.shape[1:])
        flipped = paired[:, ::-1].reshape(values.shape)
        values = jnp.where(((me >> bit) & 1) == 1, flipped, values)
    return values


def tile_table(codes, order, tiles):
    slots = codes.shape[0]
    sizes = 8 * codes * codes
    before = jnp.arange(slots)[:, None] <= jnp.arange(slots)[None, :]
    ending = jnp.sum(jnp.where(before, sizes[:, None], 0), axis=0, dtype=jnp.int32)
    number = jnp.arange(tiles, dtype=jnp.int32)
    started = (ending - sizes)[None, :] <= number[:, None]
    mine = started & (number[:, None] < ending[None, :])
    first = jnp.sum(jnp.where(mine, (ending - sizes)[None, :], 0), axis=1, dtype=jnp.int32)
    scale = jnp.sum(jnp.where(mine, codes[None, :], 0), axis=1, dtype=jnp.int32)
    width = 4 * scale
    height = 2 * scale
    local = number - first
    across = local // width
    along = local - across * width
    above = jnp.where(across > 0, number - width, -1)
    below = jnp.where(across < height - 1, number + width, -1)
    left = (along > 0).astype(jnp.int32)
    right = (along < width - 1).astype(jnp.int32)
    zero = jnp.zeros_like(number)
    return jnp.stack([above, number, below, left, right, order, zero, zero], axis=1)


def first_kernel(me_ref, x_ref, w_ref, *outs):
    step = pl.program_id(0)
    st_ref = outs[BLOCKS]
    h = dot(x_ref[0], w_ref[...])
    packed = h.astype(BF16)
    for k in range(BLOCKS):

        @pl.when(step == k)
        def _():
            outs[k][...] = packed

    part = column_sums(h, h * h)

    @pl.when(step == 0)
    def _():
        st_ref[...] = part

    @pl.when(step > 0)
    def _():
        st_ref[...] += part


def first_call(me, inputs, weight):
    rows, width = inputs.shape[1:]
    middle = weight.shape[1]
    whole = pl.BlockSpec((rows, middle), lambda b, me: (0, 0))
    return pl.pallas_call(
        first_kernel,
        grid_spec=pltpu.PrefetchScalarGridSpec(
            num_scalar_prefetch=1,
            grid=(BLOCKS,),
            in_specs=[
                pl.BlockSpec((1, rows, width), lambda b, me: (b ^ me[0], 0, 0)),
                pl.BlockSpec((width, middle), lambda b, me: (0, 0)),
            ],
            out_specs=[whole] * BLOCKS + [pl.BlockSpec((2, middle), lambda b, me: (0, 0))],
        ),
        out_shape=[jax.ShapeDtypeStruct((rows, middle), BF16)] * BLOCKS
        + [jax.ShapeDtypeStruct((2, middle), F32)],
        compiler_params=params(1),
        name="first_matmul",
    )(me, inputs, weight)


def side_mask(tab_ref, column, phases):
    mask = tab_ref[:, column : column + 1].astype(F32)
    return jnp.concatenate([mask] * phases, axis=0) if phases > 1 else mask


def onehot(column, row):
    return jnp.where(column == row, 1.0, 0.0).astype(BF16)


def shift_add(center, left, right, left_mask, right_mask):
    rows = center.shape[0]
    return (
        center
        + left_mask * pltpu.roll(left, 1, axis=0)
        + right_mask * pltpu.roll(right, rows - 1, axis=0)
    )


def conv_kernel(total, phases, nslots):
    def kernel(*refs):
        sums_ref, gain_ref, bias_ref, tab_ref, perm_ref, w_ref = refs[:6]
        slots = refs[6 : 6 + nslots]
        cols_ref, h_ref, st_ref = refs[6 + nslots : 9 + nslots]
        sends = refs[9 + nslots : 9 + 2 * nslots]
        act_ref = refs[9 + 2 * nslots]
        tiles = tab_ref.shape[0]
        each = tiles // nslots
        middle = h_ref.shape[1]
        mean, rs = moments(sums_ref[...], total)
        scale = gain_ref[...] * rs
        shift = bias_ref[...] - mean * scale
        for k in range(nslots):
            for j in range(phases):
                u = slots[k][j * each : (j + 1) * each, :].astype(F32) * scale + shift
                act_ref[k * each : (k + 1) * each, j * middle : (j + 1) * middle] = (
                    u * sigmoid(u)
                ).astype(BF16)
        row = perm_ref[...]
        for dy in range(3):
            picked = dot(onehot(tab_ref[:, dy : dy + 1], row), act_ref[...]).astype(BF16)
            for j in range(phases):
                cols_ref[j * tiles : (j + 1) * tiles, dy * middle : (dy + 1) * middle] = picked[
                    :, j * middle : (j + 1) * middle
                ]
        parts = [
            dot(cols_ref[...], w_ref[:, dx].reshape(3 * middle, middle)) for dx in range(3)
        ]
        h = shift_add(
            parts[1], parts[0], parts[2], side_mask(tab_ref, 3, phases), side_mask(tab_ref, 4, phases)
        )
        h_ref[...] = h
        st_ref[...] = column_sums(h, h * h)
        packed = h.astype(BF16)
        wide = (
            jnp.concatenate([packed[j * tiles : (j + 1) * tiles] for j in range(phases)], axis=1)
            if phases > 1
            else packed
        )
        scatter(tab_ref, wide, sends, phases)

    return kernel


def scatter(tab_ref, wide, sends, phases):
    tiles = tab_ref.shape[0]
    each = tiles // len(sends)
    middle = wide.shape[1] // phases
    row = lax.broadcasted_iota(jnp.int32, (1, tiles), 1)
    back = dot(onehot(tab_ref[:, 5:6], row), wide).astype(BF16)
    for k, send in enumerate(sends):
        for j in range(phases):
            send[j * each : (j + 1) * each, :] = back[
                k * each : (k + 1) * each, j * middle : (j + 1) * middle
            ]


def conv_call(total, phases, sums, gain, bias, table, perm, weight, slots):
    tiles = table.shape[0]
    middle = weight.shape[-1]
    n = len(slots)
    rows = phases * tiles
    slot = jax.ShapeDtypeStruct((rows // n, middle), BF16)
    return pl.pallas_call(
        conv_kernel(total, phases, n),
        out_shape=[
            jax.ShapeDtypeStruct((rows, 3 * middle), BF16),
            jax.ShapeDtypeStruct((rows, middle), F32),
            jax.ShapeDtypeStruct((2, middle), F32),
        ]
        + [slot] * n,
        scratch_shapes=[pltpu.VMEM((tiles, phases * middle), BF16)],
        compiler_params=params(),
        name="dilated_conv",
    )(sums, gain, bias, table, perm, weight, *slots)


def third_stats_kernel(total):
    def kernel(*refs):
        sums_ref, gain_ref, bias_ref, w_ref = refs[:4]
        slots = refs[4 : 4 + BLOCKS]
        act_ref, st_ref = refs[4 + BLOCKS :]
        mean, rs = moments(sums_ref[...], total)
        scale = gain_ref[...] * rs
        shift = bias_ref[...] - mean * scale
        acc = None
        for k in range(BLOCKS):
            u = slots[k][...].astype(F32) * scale + shift
            a = (u * sigmoid(u)).astype(BF16)
            act_ref[k] = a
            h = dot(a, w_ref[...])
            part = column_sums(h, h * h)
            acc = part if acc is None else acc + part
        st_ref[...] = acc

    return kernel


def third_stats_call(total, sums, gain, bias, weight, slots):
    rows, middle = slots[0].shape
    return pl.pallas_call(
        third_stats_kernel(total),
        out_shape=[
            jax.ShapeDtypeStruct((BLOCKS, rows, middle), BF16),
            jax.ShapeDtypeStruct((2, weight.shape[1]), F32),
        ],
        compiler_params=params(),
        name="third_stats",
    )(sums, gain, bias, weight, *slots)


def two_parts(value):
    high = value.astype(BF16)
    return high, (value - high.astype(F32)).astype(BF16)


def output_kernel(total):
    def kernel(me_ref, sums_ref, gain_ref, bias_ref, w_ref, a_ref, x_ref, ct_ref, y_ref, e_ref, low_ref, st_ref, *sends):
        step = pl.program_id(0)
        mean, rs = moments(sums_ref[...], total)
        h = dot(a_ref[0], w_ref[...])
        n = (h - mean) * rs
        z = gain_ref[...] * n + bias_ref[...] + x_ref[0].astype(F32)
        s = sigmoid(z)
        y = z * s
        y_ref[0] = y.astype(BF16)
        e = ct_ref[0].astype(F32) * (s + y * (1.0 - s))
        kept, low = two_parts(e * (gain_ref[...] * rs))
        e_ref[0] = kept
        low_ref[0] = low
        part = column_sums(e, e * n)

        @pl.when(step == 0)
        def _():
            st_ref[...] = part

        @pl.when(step > 0)
        def _():
            st_ref[...] += part

        raw = dot(kept, w_ref[...], ((1,), (1,))).astype(BF16)
        for k in range(BLOCKS):

            @pl.when(step == k)
            def _():
                sends[k][...] = raw

    return kernel


def output_call(total, me, sums, gain, bias, weight, act, inputs, cotangent):
    rows, middle = act.shape[1:]
    width = weight.shape[1]
    natural = pl.BlockSpec((1, rows, width), lambda b, me: (b ^ me[0], 0, 0))
    vector = pl.BlockSpec((1, width), lambda b, me: (0, 0))
    pair = pl.BlockSpec((2, width), lambda b, me: (0, 0))
    return pl.pallas_call(
        output_kernel(total),
        grid_spec=pltpu.PrefetchScalarGridSpec(
            num_scalar_prefetch=1,
            grid=(BLOCKS,),
            in_specs=[
                pair,
                vector,
                vector,
                pl.BlockSpec((middle, width), lambda b, me: (0, 0)),
                pl.BlockSpec((1, rows, middle), lambda b, me: (b, 0, 0)),
                natural,
                natural,
            ],
            out_specs=[natural, natural, natural, pair]
            + [pl.BlockSpec((rows, middle), lambda b, me: (0, 0))] * BLOCKS,
        ),
        out_shape=[jax.ShapeDtypeStruct((BLOCKS, rows, width), BF16)] * 3
        + [jax.ShapeDtypeStruct((2, width), F32)]
        + [jax.ShapeDtypeStruct((rows, middle), BF16)] * BLOCKS,
        compiler_params=params(1),
        name="block_output",
    )(me, sums, gain, bias, weight, act, inputs, cotangent)


def norm_coefficients(sums, grads, gain, total):
    mean, rs = moments(sums, total)
    keep = gain * rs
    slope = keep * rs * (grads[1:2] / total)
    offset = keep * (grads[0:1] / total) - slope * mean
    return keep, offset, slope


def third_grad_kernel(total):
    def kernel(me_ref, sums_ref, grads_ref, gain_ref, w_ref, a_ref, e_ref, low_ref, d_ref):
        _, offset, slope = norm_coefficients(sums_ref[...], grads_ref[...], gain_ref[...], total)
        h = dot(a_ref[0], w_ref[...])
        e = e_ref[0].astype(F32) + low_ref[0].astype(F32)
        d_ref[0] = (e - offset - slope * h).astype(BF16)

    return kernel


def third_grad_call(total, me, sums, grads, gain, weight, act, kept, low):
    rows, middle = act.shape[1:]
    width = weight.shape[1]
    vector = pl.BlockSpec((1, width), lambda b, me: (0, 0))
    pair = pl.BlockSpec((2, width), lambda b, me: (0, 0))
    slot = pl.BlockSpec((1, rows, width), lambda b, me: (b, 0, 0))
    return pl.pallas_call(
        third_grad_kernel(total),
        grid_spec=pltpu.PrefetchScalarGridSpec(
            num_scalar_prefetch=1,
            grid=(BLOCKS,),
            in_specs=[
                pair,
                pair,
                vector,
                pl.BlockSpec((middle, width), lambda b, me: (0, 0)),
                pl.BlockSpec((1, rows, middle), lambda b, me: (b, 0, 0)),
                pl.BlockSpec((1, rows, width), lambda b, me: (b ^ me[0], 0, 0)),
                pl.BlockSpec((1, rows, width), lambda b, me: (b ^ me[0], 0, 0)),
            ],
            out_specs=slot,
        ),
        out_shape=jax.ShapeDtypeStruct((BLOCKS, rows, width), BF16),
        compiler_params=params(1),
        name="third_grad",
    )(me, sums, grads, gain, weight, act, kept, low)


def correction_kernel(total):
    def kernel(sums3_ref, grads3_ref, gain3_ref, w_ref, sums2_ref, gain2_ref, bias2_ref, h_ref, o_ref):
        _, offset, slope = norm_coefficients(
            sums3_ref[...], grads3_ref[...], gain3_ref[...], total
        )
        w = w_ref[...]
        last = ((1,), (1,))
        high, low = two_parts(w.astype(F32) * slope)
        inner = dot(high, w, last) + dot(low, w, last)
        high, low = two_parts(inner)
        one, two = two_parts(jnp.broadcast_to(offset, (8, offset.shape[1])))
        three = (
            jnp.broadcast_to(offset, (8, offset.shape[1])) - one.astype(F32) - two.astype(F32)
        ).astype(BF16)
        constant = (dot(one, w, last) + dot(two, w, last) + dot(three, w, last))[0:1]
        mean, rs = moments(sums2_ref[...], total)
        scale = gain2_ref[...] * rs
        shift = bias2_ref[...] - mean * scale
        u = h_ref[...].astype(BF16).astype(F32) * scale + shift
        a = (u * sigmoid(u)).astype(BF16)
        o_ref[...] = constant + dot(a, high) + dot(a, low)

    return kernel


def correction_call(total, sums3, grads3, gain3, weight, sums2, gain2, bias2, hidden):
    return pl.pallas_call(
        correction_kernel(total),
        out_shape=jax.ShapeDtypeStruct(hidden.shape, F32),
        compiler_params=params(),
        name="third_grad_correction",
    )(sums3, grads3, gain3, weight, sums2, gain2, bias2, hidden)


def second_grad_kernel(total, phases, nslots):
    def kernel(*refs):
        sums_ref, gain_ref, bias_ref, tab_ref, perm_ref, h_ref, fix_ref = refs[:7]
        slots = refs[7 : 7 + nslots]
        e_ref, st_ref, wide_ref = refs[7 + nslots :]
        tiles = tab_ref.shape[0]
        each = tiles // nslots
        middle = h_ref.shape[1]
        for k in range(nslots):
            for j in range(phases):
                wide_ref[k * each : (k + 1) * each, j * middle : (j + 1) * middle] = slots[k][
                    j * each : (j + 1) * each, :
                ]
        da = dot(onehot(tab_ref[:, 1:2], perm_ref[...]), wide_ref[...])
        mean, rs = moments(sums_ref[...], total)
        acc = None
        for j in range(phases):
            n = (h_ref[j * tiles : (j + 1) * tiles, :] - mean) * rs
            u = gain_ref[...] * n + bias_ref[...]
            s = sigmoid(u)
            raw = da[:, j * middle : (j + 1) * middle] - fix_ref[j * tiles : (j + 1) * tiles, :]
            e = raw * (s * (1.0 + u * (1.0 - s)))
            e_ref[j * tiles : (j + 1) * tiles, :] = e
            part = column_sums(e, e * n)
            acc = part if acc is None else acc + part
        st_ref[...] = acc

    return kernel


def second_grad_call(total, phases, sums, gain, bias, table, perm, hidden, fix, slots):
    tiles = table.shape[0]
    rows, middle = hidden.shape
    return pl.pallas_call(
        second_grad_kernel(total, phases, len(slots)),
        out_shape=[
            jax.ShapeDtypeStruct((rows, middle), F32),
            jax.ShapeDtypeStruct((2, middle), F32),
        ],
        scratch_shapes=[pltpu.VMEM((tiles, phases * middle), BF16)],
        compiler_params=params(),
        name="second_grad",
    )(sums, gain, bias, table, perm, hidden, fix, *slots)


def conv_grad_kernel(total, phases, nslots):
    def kernel(*refs):
        sums_ref, grads_ref, gain_ref, tab_ref, h_ref, e_ref, w_ref = refs[:7]
        lefts_ref, d_ref, rights_ref = refs[7:10]
        sends = refs[10 : 10 + nslots]
        wide_ref, rows_ref = refs[10 + nslots :]
        tiles = tab_ref.shape[0]
        middle = h_ref.shape[1]
        rows = h_ref.shape[0]
        keep, offset, slope = norm_coefficients(sums_ref[...], grads_ref[...], gain_ref[...], total)
        left = side_mask(tab_ref, 3, phases)
        right = side_mask(tab_ref, 4, phases)
        d = keep * e_ref[...] - offset - slope * h_ref[...]
        packed = d.astype(BF16)
        d_ref[...] = packed
        lefts_ref[...] = (right * pltpu.roll(d, rows - 1, axis=0)).astype(BF16)
        rights_ref[...] = (left * pltpu.roll(d, 1, axis=0)).astype(BF16)
        for j in range(phases):
            wide_ref[:, j * middle : (j + 1) * middle] = packed[j * tiles : (j + 1) * tiles]
            rows_ref[j * tiles : (j + 1) * tiles, middle : 2 * middle] = packed[
                j * tiles : (j + 1) * tiles
            ]
        row = lax.broadcasted_iota(jnp.int32, (1, tiles), 1)
        for dy in (0, 2):
            picked = dot(onehot(tab_ref[:, dy : dy + 1], row), wide_ref[...]).astype(BF16)
            for j in range(phases):
                rows_ref[j * tiles : (j + 1) * tiles, dy * middle : (dy + 1) * middle] = picked[
                    :, j * middle : (j + 1) * middle
                ]
        parts = []
        for dx in range(3):
            part = None
            for dy in range(3):
                term = dot(
                    rows_ref[:, dy * middle : (dy + 1) * middle], w_ref[2 - dy, 2 - dx], ((1,), (1,))
                )
                part = term if part is None else part + term
            parts.append(part)
        da = shift_add(parts[1], parts[0], parts[2], left, right).astype(BF16)
        for j in range(phases):
            wide_ref[:, j * middle : (j + 1) * middle] = da[j * tiles : (j + 1) * tiles]
        scatter(tab_ref, wide_ref[...], sends, phases)

    return kernel


def conv_grad_call(total, phases, nslots, sums, grads, gain, table, hidden, e, weight):
    tiles = table.shape[0]
    rows, middle = hidden.shape
    slot = jax.ShapeDtypeStruct((rows // nslots, middle), BF16)
    return pl.pallas_call(
        conv_grad_kernel(total, phases, nslots),
        out_shape=[jax.ShapeDtypeStruct((rows, middle), BF16)] * 3 + [slot] * nslots,
        scratch_shapes=[
            pltpu.VMEM((tiles, phases * middle), BF16),
            pltpu.VMEM((rows, 3 * middle), BF16),
        ],
        compiler_params=params(),
        name="dilated_conv_grad",
    )(sums, grads, gain, table, hidden, e, weight)


def first_grad_kernel(total):
    def kernel(*refs):
        sums_ref, gain_ref, bias_ref = refs[:3]
        grads = refs[3 : 3 + BLOCKS]
        hiddens = refs[3 + BLOCKS : 3 + 2 * BLOCKS]
        e_ref, st_ref = refs[3 + 2 * BLOCKS :]
        mean, rs = moments(sums_ref[...], total)
        acc = None
        for k in range(BLOCKS):
            n = (hiddens[k][...].astype(F32) - mean) * rs
            u = gain_ref[...] * n + bias_ref[...]
            s = sigmoid(u)
            e = grads[k][...].astype(F32) * (s * (1.0 + u * (1.0 - s)))
            e_ref[k] = e
            part = column_sums(e, e * n)
            acc = part if acc is None else acc + part
        st_ref[...] = acc

    return kernel


def first_grad_call(total, sums, gain, bias, grads, hiddens):
    rows, middle = hiddens[0].shape
    return pl.pallas_call(
        first_grad_kernel(total),
        out_shape=[
            jax.ShapeDtypeStruct((BLOCKS, rows, middle), F32),
            jax.ShapeDtypeStruct((2, middle), F32),
        ],
        compiler_params=params(),
        name="first_grad",
    )(sums, gain, bias, *grads, *hiddens)


def first_hidden_grad_kernel(total):
    def kernel(me_ref, sums_ref, grads_ref, gain_ref, e_ref, *refs):
        hiddens = refs[:BLOCKS]
        d_ref = refs[BLOCKS]
        keep, offset, slope = norm_coefficients(sums_ref[...], grads_ref[...], gain_ref[...], total)
        for k in range(BLOCKS):
            d = keep * e_ref[k] - offset - slope * hiddens[k][...].astype(F32)
            d_ref[k ^ me_ref[0]] = d.astype(BF16)

    return kernel


def first_hidden_grad_call(total, me, sums, grads, gain, e, hiddens):
    rows, middle = hiddens[0].shape
    vmem = pl.BlockSpec(memory_space=pltpu.VMEM)
    return pl.pallas_call(
        first_hidden_grad_kernel(total),
        in_specs=[pl.BlockSpec(memory_space=pltpu.SMEM)] + [vmem] * (4 + BLOCKS),
        out_specs=vmem,
        out_shape=jax.ShapeDtypeStruct((BLOCKS, rows, middle), BF16),
        compiler_params=params(),
        name="first_hidden_grad",
    )(me, sums, grads, gain, e, *hiddens)


def input_grad_kernel(total):
    def kernel(sums_ref, gain_ref, d_ref, w_ref, e_ref, o_ref):
        _, rs = moments(sums_ref[...], total)
        undo = 1.0 / (gain_ref[...] * rs)
        o_ref[0] = dot(d_ref[0], w_ref[...], ((1,), (1,))) + e_ref[0].astype(F32) * undo

    return kernel


def input_grad_call(total, sums, gain, d, weight, kept):
    rows, middle = d.shape[1:]
    width = weight.shape[0]
    return pl.pallas_call(
        input_grad_kernel(total),
        grid=(BLOCKS,),
        in_specs=[
            pl.BlockSpec((2, width), lambda b: (0, 0)),
            pl.BlockSpec((1, width), lambda b: (0, 0)),
            pl.BlockSpec((1, rows, middle), lambda b: (b, 0, 0)),
            pl.BlockSpec((width, middle), lambda b: (0, 0)),
            pl.BlockSpec((1, rows, width), lambda b: (b, 0, 0)),
        ],
        out_specs=pl.BlockSpec((1, rows, width), lambda b: (b, 0, 0)),
        out_shape=jax.ShapeDtypeStruct((BLOCKS, rows, width), F32),
        compiler_params=params(1),
        name="input_grad",
    )(sums, gain, d, weight, kept)


def swap(value, mask, count):
    return lax.ppermute(value, AXES, [(i, i ^ mask) for i in range(count)])


def small_sum(value, count):
    if count != 32:
        return lax.psum(value, AXES)
    for masks in ((1,), (2, 4, 6), (8, 16, 24)):
        arrived = [value] + [swap(value, m, count) for m in masks]
        while len(arrived) > 1:
            arrived = [a + b for a, b in zip(arrived[::2], arrived[1::2])]
        value = arrived[0]
    return value


def by_bits(values, place, bits):
    for bit in range(bits):
        paired = values.reshape((1 << (bits - bit - 1), 2, 1 << bit) + values.shape[1:])
        flipped = paired[:, ::-1].reshape(values.shape)
        values = jnp.where(((place >> bit) & 1) == 1, flipped, values)
    return values


def scatter_sum(value, stages, index, count):
    for shift, bits in stages:
        n = 1 << bits
        mine = (index >> shift) & (n - 1)
        parts = value.reshape((n, value.shape[0] // n) + value.shape[1:])
        kept = lax.dynamic_index_in_dim(parts, mine, 0, keepdims=False).astype(F32)
        for m in range(1, n):
            leaving = lax.dynamic_index_in_dim(parts, mine ^ m, 0, keepdims=False)
            kept = kept + swap(leaving, m << shift, count).astype(F32)
        value = kept.astype(BF16)
    return value


def gather_back(value, stages, index, count):
    for shift, bits in stages[::-1]:
        n = 1 << bits
        arrived = [value] + [swap(value, m << shift, count) for m in range(1, n)]
        value = by_bits(jnp.stack(arrived), (index >> shift) & (n - 1), bits)
        value = value.reshape((n * value.shape[1],) + value.shape[2:])
    return value


STAGES = (((0, 1), (1, 1), (2, 1), (3, 2)), ((0, 1), (2, 1), (1, 1), (3, 2)))


def weight_sum(value, index, count):
    if count != 32:
        return lax.psum(value.astype(F32), AXES)
    halves = value.reshape((2, value.shape[0] // 2) + value.shape[1:])
    out = [
        gather_back(scatter_sum(halves[i], STAGES[i], index, count), STAGES[i], index, count)
        for i in range(2)
    ]
    return jnp.concatenate(out, axis=0).astype(F32)


SEND_ORDER = (6, 7, 4, 5, 2, 3, 1)


def exchange_slots(slots):
    out = [slots[0]] + [None] * (BLOCKS - 1)
    for k in SEND_ORDER:
        out[k] = lax.ppermute(slots[k], "dp", [(i, i ^ k) for i in range(BLOCKS)])
    return out


def body(
    block_in,
    crop_codes,
    tile_perm,
    reduce_weight,
    dilated_weight,
    expand_weight,
    first_gain,
    first_bias,
    middle_gain,
    middle_bias,
    last_gain,
    last_bias,
    cotangent,
):
    devices = lax.axis_size("dp")
    replicas = lax.axis_size("rep")
    count = devices * replicas
    sets = crop_codes.shape[1]
    phases = 16 * sets // devices
    pixels, width = block_in.shape[1:]
    middle = reduce_weight.shape[1]
    tiles = tile_perm.shape[2]
    each = tiles // devices
    rows = pixels // BLOCKS
    total = float(pixels * count)
    paired = devices == BLOCKS

    place = lax.axis_index("dp").astype(jnp.int32)
    me = (place if paired else jnp.zeros_like(place)).reshape(1)
    set_index = place * phases // 16
    codes = lax.dynamic_index_in_dim(crop_codes[0], set_index, 0, keepdims=False)
    order = lax.dynamic_index_in_dim(tile_perm[0], set_index, 0, keepdims=False)
    if paired:
        order = xor_blocks(order.reshape(BLOCKS, each), place).reshape(tiles)
    table = tile_table(codes, order, tiles)
    perm = order.reshape(1, tiles)

    def to_phases(slots):
        if paired:
            return exchange_slots(slots)
        joined = jnp.concatenate(slots, axis=0).reshape(devices, phases, each, middle)
        moved = lax.all_to_all(joined, "dp", split_axis=0, concat_axis=2, tiled=True)
        return [moved.reshape(phases * tiles, middle)]

    def to_pixels(slots):
        if paired:
            return exchange_slots(slots)
        parted = slots[0].reshape(phases, devices, each, middle)
        moved = lax.all_to_all(parted, "dp", split_axis=1, concat_axis=0, tiled=True)
        moved = moved.reshape(BLOCKS, rows, middle)
        return [moved[k] for k in range(BLOCKS)]

    flat = block_in[0]
    inputs = flat.reshape(BLOCKS, rows, width)
    upstream = cotangent[0].reshape(BLOCKS, rows, width)
    taps = dilated_weight.reshape(3, 3, middle, middle)
    gain1, bias1 = first_gain.reshape(1, middle), first_bias.reshape(1, middle)
    gain2, bias2 = middle_gain.reshape(1, middle), middle_bias.reshape(1, middle)
    gain3, bias3 = last_gain.reshape(1, width), last_bias.reshape(1, width)

    *hidden1, part = first_call(me, inputs, reduce_weight)
    slots = to_phases(hidden1)
    sums1 = small_sum(part, count)
    columns, hidden2, part, *slots = conv_call(
        total, phases, sums1, gain1, bias1, table, perm, taps, slots
    )
    nslots = len(slots)
    slots = to_pixels(slots)
    sums2 = small_sum(part, count)
    act2, part = third_stats_call(total, sums2, gain2, bias2, expand_weight, slots)
    sums3 = small_sum(part, count)
    block_out, kept, low, part, *slots = output_call(
        total, me, sums3, gain3, bias3, expand_weight, act2, inputs, upstream
    )
    slots = to_phases(slots)
    grads3 = small_sum(part, count)
    fix = correction_call(
        total, sums3, grads3, gain3, expand_weight, sums2, gain2, bias2, hidden2
    )
    grad3 = third_grad_call(total, me, sums3, grads3, gain3, expand_weight, act2, kept, low)
    expand_grad = dot(
        act2.reshape(pixels, middle), grad3.reshape(pixels, width), ((0,), (0,))
    )
    slots, expand_grad = lax.optimization_barrier((slots, expand_grad))
    e2, part = second_grad_call(
        total, phases, sums2, gain2, bias2, table, perm, hidden2, fix, slots
    )
    grads2 = small_sum(part, count)
    *shifted, = conv_grad_call(
        total, phases, nslots, sums2, grads2, gain2, table, hidden2, e2, taps
    )
    shifted, slots = shifted[:3], shifted[3:]
    slots = to_pixels(slots)
    dilated_grad = jnp.concatenate(
        [dot(columns, d, ((0,), (0,))).astype(BF16) for d in shifted], axis=0
    )
    e1, part = first_grad_call(total, sums1, gain1, bias1, slots, hidden1)
    grads1 = small_sum(part, count)
    grad1 = first_hidden_grad_call(total, me, sums1, grads1, gain1, e1, hidden1)
    reduce_grad = dot(flat, grad1.reshape(pixels, middle), ((0,), (0,))).astype(BF16)
    grad_in = input_grad_call(total, sums3, gain3, grad1, reduce_weight, kept)
    index = place * replicas + lax.axis_index("rep").astype(jnp.int32)
    expand_grad = lax.psum(expand_grad, AXES)
    dilated_grad = weight_sum(dilated_grad, index, count)
    dilated_grad = (
        dilated_grad.reshape(3, 3, middle, middle).transpose(1, 0, 2, 3).reshape(9 * middle, middle)
    )
    reduce_grad = weight_sum(reduce_grad, index, count)
    return (
        block_out.reshape(1, pixels, width),
        grad_in.reshape(1, pixels, width),
        reduce_grad,
        dilated_grad,
        expand_grad,
        grads1[1],
        grads1[0],
        grads2[1],
        grads2[0],
        grads3[1],
        grads3[0],
    )


def solution(mesh):
    in_specs = (
        P("rep", "dp", None),
        P("rep", None, None),
        P("rep", None, None),
        P(),
        P(),
        P(),
        P(),
        P(),
        P(),
        P(),
        P(),
        P(),
        P("rep", "dp", None),
    )
    out_specs = (P("rep", "dp", None),) * 2 + (P(),) * 9
    return jax.shard_map(body, mesh=mesh, in_specs=in_specs, out_specs=out_specs, check_vma=False)
```

time: 1240 us -> 549 us (0.44)
  local copies, waits for them, and re-layouts: 370 us -> 27.5 us
  blocking collectives: 276 us -> 0 us
  waiting for transfers between devices: 360 us -> 140 us
  starting transfers between devices: 16.4 us -> 160 us
  Pallas kernels: 0 us -> 134 us
  other arithmetic: 101 us -> 31 us
  matrix products: 88.3 us -> 30.7 us
    psum x1, waiting for transfers between devices: 282 us -> 0.01 us  [body(): expand_grad = lax.psum(expand_grad, AXES)]
    psum x6 -> x0, blocking collectives: 235 us -> none  [the longest x3 119 us: norm_forward(): lax.psum((jnp.sum(hidden, axis=0), jnp.sum(hidden * hidden, axis=0)), ('d...]
    gather x15 -> x0, local copies, waits for them, and re-layouts: 196 us -> none  [the longest x2 87.2 us: body(): columns = jnp.take(padded, neighbors, axis=1).reshape(pixels, 9 * middle)]
    ppermute x0 -> x118, starting transfers between devices: none -> 160 us  [the longest x90 111 us: swap(): return lax.ppermute(value, AXES, [(i, i ^ mask) for i in range(count)])]
    ppermute x0 -> x118, waiting for transfers between devices: none -> 140 us  [the longest x90 90 us: swap(): return lax.ppermute(value, AXES, [(i, i ^ mask) for i in range(count)])]
    pallas_call x0 -> x11, Pallas kernels: none -> 134 us  [the longest x1 25.6 us: output_call(): pl.pallas_call(output_kernel(total), grid_spec=pltpu.PrefetchScalarGridSp...]
    squeeze x10 -> x16, local copies, waits for them, and re-layouts: 101 us -> 5.52 us  [scatter_sum(): leaving = lax.dynamic_index_in_dim(parts, mine ^ m, 0, keepdims=False)]
    all_to_all x3 -> x0, waiting for transfers between devices: 77.2 us -> none  [the longest x1 35.8 us: body(): lax.all_to_all(grad_act_two.reshape(devices, phase_dev, per_device, middl...]
  transfers between devices with their start and end apart: 4 -> 119, of which waited for: 4 -> 53; matrix products, arithmetic and copies ran while one was open for 3% -> 14% of each run, Pallas kernels for 0% -> 12%
where the time goes in v1:
time: 549 us; the launch traced here: 538 us
  starting transfers between devices  160 us (29%)
  waiting for transfers between devices  140 us (26%)
  Pallas kernels  134 us (24%)
  other arithmetic  31 us (6%)
  matrix products  30.7 us (6%)
  local copies, waits for them, and re-layouts  27.5 us (5%)
  between operations  15.5 us (3%)
    ppermute x90, starting transfers between devices, swap(): return lax.ppermute(value, AXES, [(i, i ^ mask) for i in range(count)])  111 us
    ppermute x90, waiting for transfers between devices, swap(): return lax.ppermute(value, AXES, [(i, i ^ mask) for i in range(count)])  90 us
    ppermute x28, waiting for transfers between devices, exchange_slots(): out[k] = lax.ppermute(slots[k], 'dp', [(i, i ^ k) for i in range(BLOCKS)])  50.4 us
    ppermute x28, starting transfers between devices, exchange_slots(): out[k] = lax.ppermute(slots[k], 'dp', [(i, i ^ k) for i in range(BLOCKS)])  48.6 us
    dot_general x5, matrix products, dot(): return lax.dot_general(a, b, (dims, ((), ())), preferred_element_type=F32)  30.7 us
    pallas_call x1, Pallas kernels, output_call(): pl.pallas_call(output_kernel(total), grid_spec=pltpu.PrefetchScalarGridSp...  25.6 us
    pallas_call x1, Pallas kernels, conv_grad_call(): pl.pallas_call(conv_grad_kernel(total, phases, nslots), out_shape=[jax.Sh...  19.2 us
    pallas_call x1, Pallas kernels, conv_call(): pl.pallas_call(conv_kernel(total, phases, n), out_shape=[jax.ShapeDtypeSt...  19 us
  transfers between devices with their start and end apart: 119, of which 53 were waited for; matrix products, arithmetic and copies ran while one was open for 14% of the time, Pallas kernels for 12%

profile of v1, /device:TPU:0, one launch (start us, length us, event | category | flops | bytes accessed | tf_op | source)
XLA Modules:
  0.0 538.3 jit_solution(951550144967738253)
XLA Ops:
  7.2 10.2 %first_matmul.1 = (bf16[192,512]{1,0:T(8,128)(2,1)}, bf16[192,512]{1,0:T(8,128)(2,1)}, bf16[192,512]{1,0:T(8,128)(2,1)}, bf16[192,512]{1,0:T(8,128)(2,1)}, bf16[...) custom-call(s32[1]{0:T(128)} %bitcast.me_ref, ...), custom_call_target="tpu_custom_call" | custom-call | tf_op jit(solution)/shard_map/first_matmul/pallas_call | solution.py:100
  46.1 15.5 %collective-permute-done.10.refs_10_ = bf16[192,512]{1,0:T(8,128)(2,1)S(1)} collective-permute-done((bf16[192,512]{1,0:T(8,128)(2,1)}, bf16[192,512]{1,0:T(8,128)(2,1)S(1)}, u32[]{:S(2)}, u32[]{:S(2)}) %collective-permute-start.10) | collective-permute-done | bytes 196640 | tf_op jit(solution)/shard_map/ppermute | solution.py:658
  67.1 19.0 %dilated_conv.1 = (bf16[1536,1536]{1,0:T(8,128)(2,1)}, f32[1536,512]{1,0:T(8,128)}, f32[2,512]{1,0:T(2,128)}, bf16[192,512]{1,0:T(8,128)(2,1)}, bf16[192,512]{1,...) custom-call(f32[2,512]{1,0:T(2,128)} %add_add_fusion.10.refs_0_.sums, ...), custom_call_target="tpu_custom_call" | custom-call | tf_op jit(solution)/shard_map/dilated_conv/pallas_call | solution.py:200
  92.7 6.5 %collective-permute-start.22 = (bf16[192,512]{1,0:T(8,128)(2,1)}, bf16[192,512]{1,0:T(8,128)(2,1)S(1)}, u32[]{:S(2)}, u32[]{:S(2)}) collective-permute-start(bf16[192,512]{1,0:T(8,128)(2,1)} %get-tuple-element.81), channel_id=1, source_target_pairs={{0,8},{4,12},{8,0},{12,4},{16,24},{20,28},{24,16},{28,20},{1,9},{5... | collective-permute-start | bytes 589832 | tf_op jit(solution)/shard_map/ppermute | solution.py:658
  114.5 16.3 %collective-permute-done.24.refs_8_ = bf16[192,512]{1,0:T(8,128)(2,1)S(1)} collective-permute-done((bf16[192,512]{1,0:T(8,128)(2,1)}, bf16[192,512]{1,0:T(8,128)(2,1)S(1)}, u32[]{:S(2)}, u32[]{:S(2)}) %collective-permute-start.24) | collective-permute-done | bytes 196640 | tf_op jit(solution)/shard_map/ppermute | solution.py:658
  136.3 6.7 %third_stats.1 = (bf16[8,192,512]{2,1,0:T(8,128)(2,1)}, f32[2,2048]{1,0:T(2,128)}) custom-call(f32[2,512]{1,0:T(2,128)} %add_add_fusion.8.refs_0_.sums2_ref, f32[1,512]{1,0:T(1,128)} %bitcast.413, f32[1,512]{1,0:T(1,128)} %bitcast.420, bf16[512,2048]{1,0:T(8,128)(2,1)} %w_ref.8, bf16[192,512]{1,0:T(8,128)(2,1)} %get-tuple-element.79.refs_4_, ...), custom_call_target="tpu_custom_call" | custom-call | tf_op jit(solution)/shard_map/third_stats/pallas_call | solution.py:237
  152.6 6.5 %collective-permute-start.33 = (f32[2,2048]{1,0:T(2,128)S(1)}, f32[2,2048]{1,0:T(2,128)S(1)}, u32[]{:S(2)}, u32[]{:S(2)}) collective-permute-start(f32[2,2048]{1,0:T(2,128)S(1)} %add_add_fusion.3), channel_id=1, source_target_pairs={{0,16},{1,17},{2,18},{3,19},{4,20},{5,21},{6,22},{7,23},{8,24},{9,... | collective-permute-start | bytes 49160 | tf_op jit(solution)/shard_map/ppermute | solution.py:594
  163.5 25.6 %block_output.1 = (bf16[8,192,2048]{2,1,0:T(8,128)(2,1)}, bf16[8,192,2048]{2,1,0:T(8,128)(2,1)}, bf16[8,192,2048]{2,1,0:T(8,128)(2,1)}, f32[2,2048]{1,0:T(2,128)...) custom-call(s32[1]{0:T(128)} %bitcast.me_ref, ...), custom_call_target="tpu_custom_call" | custom-call | tf_op jit(solution)/shard_map/block_output/pallas_call | solution.py:293
  209.7 12.8 %third_grad.1 = bf16[8,192,2048]{2,1,0:T(8,128)(2,1)} custom-call(s32[1]{0:T(128)} %bitcast.me_ref, f32[2,2048]{1,0:T(2,128)} %add_add_fusion.2.sums_ref.sums3_ref, f32[2,2048]{1,0:T(2,128)} %add_add_fusion.grads3_ref.grads_ref, f32[1,2048]{1,0:T(1,128)} %bitcast.397, bf16[512,2048]{1,0:T(8,128)(2,1)} %w_ref.8, ...), custom_call_target="tpu_custom_call" | custom-call | tf_op jit(solution)/shard_map/third_grad/pallas_call | solution.py:342
  227.2 7.9 %convolution_bitcast_fusion = f32[512,2048]{1,0:T(8,128)} fusion(bf16[8,192,512]{2,1,0:T(8,128)(2,1)S(1)} %copy-done.2, bf16[8,192,2048]{2,1,0:T(8,128)(2,1)} %third_grad.1), kind=kOutput, calls=%fused_computation.6 | convolution fusion | flops 3221225472 | bytes 12058624 | tf_op jit(solution)/shard_map/dot_general | solution.py:28
  235.1 10.0 %third_grad_correction.1.refs_6_ = f32[1536,512]{1,0:T(8,128)} custom-call(f32[2,2048]{1,0:T(2,128)} %add_add_fusion.2.sums_ref.sums3_ref, f32[2,2048]{1,0:T(2,128)} %add_add_fusion.grads3_ref.grads_ref, f32[1,2048]{1,0:T(1,128)} %bitcast.398, bf16[512,2048]{1,0:T(8,128)(2,1)} %w_ref.8, f32[2,512]{1,0:T(2,128)} %add_add_fusion.8.refs_0_.sums2_ref, ...), custom_call_target="tpu_custom_call" | custom-call | tf_op jit(solution)/shard_map/third_grad_correction/pallas_call | solution.py:390
  246.0 7.6 %second_grad.1 = (f32[1536,512]{1,0:T(8,128)}, f32[2,512]{1,0:T(2,128)}) custom-call(f32[2,512]{1,0:T(2,128)} %add_add_fusion.8.refs_0_.sums2_ref, f32[1,512]{1,0:T(1,128)} %bitcast.415, f32[1,512]{1,0:T(1,128)} %bitcast.422, s32[768,8]{1,0:T(8,128)} %copy.75.refs_3_, s32[1,768]{1,0:T(1,128)} %broadcast_select_fusion.2.refs_4_, ...), custom_call_target="tpu_custom_call" | custom-call | tf_op jit(solution)/shard_map/second_grad/pallas_call | solution.py:431
  268.2 19.2 %dilated_conv_grad.1 = (bf16[1536,512]{1,0:T(8,128)(2,1)}, bf16[1536,512]{1,0:T(8,128)(2,1)}, bf16[1536,512]{1,0:T(8,128)(2,1)}, bf16[192,512]{1,0:T(8,128)(2,1)...) custom-call(f32[2,512]{1,0:T(2,128)} %add_add_fusion.8.refs_0_.sums2, ...), custom_call_target="tpu_custom_call" | custom-call | tf_op jit(solution)/shard_map/dilated_conv_grad/pallas_call | solution.py:493
  294.4 5.6 %convolution_convert_fusion.2 = bf16[1536,512]{1,0:T(8,128)(2,1)S(1)} fusion(bf16[1536,1536]{1,0:T(8,128)(2,1)} %get-tuple-element.122, bf16[1536,512]{1,0:T(8,128)(2,1)} %get-tuple-element.123), kind=kOutput, calls=%fused_computation.10 | convolution fusion | flops 2416705536 | bytes 7864320 | tf_op jit(solution)/shard_map/dot_general | solution.py:28
  300.1 6.3 %convolution_convert_fusion.1 = bf16[1536,512]{1,0:T(8,128)(2,1)} fusion(bf16[1536,1536]{1,0:T(8,128)(2,1)} %get-tuple-element.122, bf16[1536,512]{1,0:T(8,128)(2,1)S(1)} %copy-done.41), kind=kOutput, calls=%fused_computation.9 | convolution fusion | flops 2416705536 | bytes 7864320 | tf_op jit(solution)/shard_map/dot_general | solution.py:28
  323.7 5.5 %first_grad.1 = (f32[8,192,512]{2,1,0:T(8,128)}, f32[2,512]{1,0:T(2,128)}) custom-call(f32[2,512]{1,0:T(2,128)} %add_add_fusion.10.refs_0_.sums_ref, f32[1,512]{1,0:T(1,128)} %bitcast.418, f32[1,512]{1,0:T(1,128)} %bitcast.427, bf16[192,512]{1,0:T(8,128)(2,1)} %get-tuple-element.112.refs_3_, bf16[192,512]{1,0:T(8,128)(2,1)} %copy-done.14, ...), custom_call_target="tpu_custom_call" | custom-call | tf_op jit(solution)/shard_map/first_grad/pallas_call | solution.py:528
  339.8 8.1 %collective-permute-start.68 = (f32[2,512]{1,0:T(2,128)S(1)}, f32[2,512]{1,0:T(2,128)S(1)}, u32[]{:S(2)}, u32[]{:S(2)}) collective-permute-start(f32[2,512]{1,0:T(2,128)S(1)} %add_add_fusion.5), channel_id=1, source_target_pairs={{0,16},{1,17},{2,18},{3,19},{4,20},{5,21},{6,22},{7,23},{8,24},{9,... | collective-permute-start | bytes 12296 | tf_op jit(solution)/shard_map/ppermute | solution.py:594
  356.1 6.8 %fusion.5 = bf16[2048,512]{0,1:T(8,128)(2,1)S(1)} fusion(bf16[1536,512]{1,0:T(8,128)(2,1)} %bitcast.329, bf16[1,1536,2048]{2,1,0:T(8,128)(2,1)} %param.13), kind=kOutput, calls=%fused_computation.11 | convolution fusion | flops 3222274048 | bytes 9961472 | tf_op jit(solution)/shard_map/dot_general | solution.py:28
  367.4 13.0 %input_grad.1 = f32[8,192,2048]{2,1,0:T(8,128)} custom-call(f32[2,2048]{1,0:T(2,128)} %add_add_fusion.2.sums_ref.sums3_ref, f32[1,2048]{1,0:T(1,128)} %bitcast.399, bf16[8,192,512]{2,1,0:T(8,128)(2,1)} %first_hidden_grad.1.d_ref, bf16[2048,512]{1,0:T(8,128)(2,1)} %w_ref.9, bf16[8,192,2048]{2,1,0:T(8,128)(2,1)} %get-tuple-element.100.e_ref), custom_call_target="tpu_custom_call" | custom-call | tf_op jit(solution)/shard_map/input_grad/pallas_call | solution.py:576
  388.6 6.4 %collective-permute-done.71 = bf16[256,512]{1,0:T(8,128)(2,1)S(1)} collective-permute-done((bf16[256,512]{1,0:T(8,128)(2,1)S(1)}, bf16[256,512]{1,0:T(8,128)(2,1)S(1)}, u32[]{:S(2)}, u32[]{:S(2)}) %collective-permute-start.71) | collective-permute-done | bytes 262176 | tf_op jit(solution)/shard_map/ppermute | solution.py:594
  432.7 9.2 %collective-permute-done.79 = bf16[128,512]{1,0:T(8,128)(2,1)S(1)} collective-permute-done((bf16[128,512]{1,0:T(8,128)(2,1)S(1)}, bf16[128,512]{1,0:T(8,128)(2,1)S(1)}, u32[]{:S(2)}, u32[]{:S(2)}) %collective-permute-start.79) | collective-permute-done | bytes 131104 | tf_op jit(solution)/shard_map/ppermute | solution.py:594
  457.0 6.4 %collective-permute-done.96 = bf16[288,512]{1,0:T(8,128)(2,1)S(1)} collective-permute-done((bf16[288,512]{1,0:T(8,128)(2,1)S(1)}, bf16[288,512]{1,0:T(8,128)(2,1)S(1)}, u32[]{:S(2)}, u32[]{:S(2)}) %collective-permute-start.96) | collective-permute-done | bytes 294944 | tf_op jit(solution)/shard_map/ppermute | solution.py:594
  497.5 6.4 %collective-permute-done.115 = bf16[288,512]{1,0:T(8,128)(2,1)S(1)} collective-permute-done((bf16[288,512]{1,0:T(8,128)(2,1)S(1)}, bf16[288,512]{1,0:T(8,128)(2,1)S(1)}, u32[]{:S(2)}, u32[]{:S(2)}) %collective-permute-start.115) | collective-permute-done | bytes 294944 | tf_op jit(solution)/shard_map/ppermute | solution.py:594
  505.2 7.6 %collective-permute-done.104 = bf16[576,512]{1,0:T(8,128)(2,1)S(1)} collective-permute-done((bf16[576,512]{1,0:T(8,128)(2,1)S(1)}, bf16[576,512]{1,0:T(8,128)(2,1)S(1)}, u32[]{:S(2)}, u32[]{:S(2)}) %collective-permute-start.104) | collective-permute-done | bytes 589856 | tf_op jit(solution)/shard_map/ppermute | solution.py:594
  (465 shorter events, 277.8 us)
Async XLA Ops:
  7.2 519.4 %all-reduce.2.cloned.1.call-start = ((), (), s32[]{:S(2)}) async-start(), calls=%async_computation | async-start | bytes 8388608 | tf_op jit(solution)/shard_map/psum | solution.py:765
  17.9 22.9 %collective-permute-start.7 = (bf16[192,512]{1,0:T(8,128)(2,1)}, bf16[192,512]{1,0:T(8,128)(2,1)S(1)}, u32[]{:S(2)}, u32[]{:S(2)}) collective-permute-start(bf16[192,512]{1,0:T(8,128)(2,1)} %get-tuple-element.71.refs_12_.refs_1_), channel_id=1, source_target_pairs={{0,4},{4,0},{8,12},{12,8},{16,20},{20,16},{24,28},{28,24},{1,5},{5... | collective-permute-start | bytes 589832 | tf_op jit(solution)/shard_map/ppermute | solution.py:658
  20.4 23.0 %collective-permute-start.8 = (bf16[192,512]{1,0:T(8,128)(2,1)}, bf16[192,512]{1,0:T(8,128)(2,1)S(1)}, u32[]{:S(2)}, u32[]{:S(2)}) collective-permute-start(bf16[192,512]{1,0:T(8,128)(2,1)} %get-tuple-element.72.refs_13_.refs_2_), channel_id=1, source_target_pairs={{0,8},{4,12},{8,0},{12,4},{16,24},{20,28},{24,16},{28,20},{1,9},{5... | collective-permute-start | bytes 589832 | tf_op jit(solution)/shard_map/ppermute | solution.py:658
  37.8 23.8 %collective-permute-start.10 = (bf16[192,512]{1,0:T(8,128)(2,1)}, bf16[192,512]{1,0:T(8,128)(2,1)S(1)}, u32[]{:S(2)}, u32[]{:S(2)}) collective-permute-start(bf16[192,512]{1,0:T(8,128)(2,1)} %get-tuple-element.74.refs_15_.refs_4_), channel_id=1, source_target_pairs={{0,16},{4,20},{8,24},{12,28},{16,0},{20,4},{24,8},{28,12},{1,17},{... | collective-permute-start | bytes 589832 | tf_op jit(solution)/shard_map/ppermute | solution.py:658
  39.4 26.8 %collective-permute-start.11 = (bf16[192,512]{1,0:T(8,128)(2,1)}, bf16[192,512]{1,0:T(8,128)(2,1)S(1)}, u32[]{:S(2)}, u32[]{:S(2)}) collective-permute-start(bf16[192,512]{1,0:T(8,128)(2,1)} %get-tuple-element.75.refs_16_.refs_5_), channel_id=1, source_target_pairs={{0,20},{4,16},{8,28},{12,24},{16,4},{20,0},{24,12},{28,8},{1,21},{... | collective-permute-start | bytes 589832 | tf_op jit(solution)/shard_map/ppermute | solution.py:658
  40.7 25.5 %collective-permute-start.12 = (bf16[192,512]{1,0:T(8,128)(2,1)}, bf16[192,512]{1,0:T(8,128)(2,1)S(1)}, u32[]{:S(2)}, u32[]{:S(2)}) collective-permute-start(bf16[192,512]{1,0:T(8,128)(2,1)} %get-tuple-element.76.refs_17_.refs_6_), channel_id=1, source_target_pairs={{0,24},{4,28},{8,16},{12,20},{16,8},{20,12},{24,0},{28,4},{1,25},{... | collective-permute-start | bytes 589832 | tf_op jit(solution)/shard_map/ppermute | solution.py:658
  43.5 22.8 %collective-permute-start.13 = (bf16[192,512]{1,0:T(8,128)(2,1)}, bf16[192,512]{1,0:T(8,128)(2,1)S(1)}, u32[]{:S(2)}, u32[]{:S(2)}) collective-permute-start(bf16[192,512]{1,0:T(8,128)(2,1)} %get-tuple-element.77.refs_18_.refs_7_), channel_id=1, source_target_pairs={{0,28},{4,24},{8,20},{12,16},{16,12},{20,8},{24,4},{28,0},{1,29},{... | collective-permute-start | bytes 589832 | tf_op jit(solution)/shard_map/ppermute | solution.py:658
  105.9 25.0 %collective-permute-start.24 = (bf16[192,512]{1,0:T(8,128)(2,1)}, bf16[192,512]{1,0:T(8,128)(2,1)S(1)}, u32[]{:S(2)}, u32[]{:S(2)}) collective-permute-start(bf16[192,512]{1,0:T(8,128)(2,1)} %get-tuple-element.83), channel_id=1, source_target_pairs={{0,16},{4,20},{8,24},{12,28},{16,0},{20,4},{24,8},{28,12},{1,17},{... | collective-permute-start | bytes 589832 | tf_op jit(solution)/shard_map/ppermute | solution.py:658
  108.3 27.2 %collective-permute-start.25 = (bf16[192,512]{1,0:T(8,128)(2,1)}, bf16[192,512]{1,0:T(8,128)(2,1)S(1)}, u32[]{:S(2)}, u32[]{:S(2)}) collective-permute-start(bf16[192,512]{1,0:T(8,128)(2,1)} %get-tuple-element.84), channel_id=1, source_target_pairs={{0,20},{4,16},{8,28},{12,24},{16,4},{20,0},{24,12},{28,8},{1,21},{... | collective-permute-start | bytes 589832 | tf_op jit(solution)/shard_map/ppermute | solution.py:658
  109.8 25.8 %collective-permute-start.26 = (bf16[192,512]{1,0:T(8,128)(2,1)}, bf16[192,512]{1,0:T(8,128)(2,1)S(1)}, u32[]{:S(2)}, u32[]{:S(2)}) collective-permute-start(bf16[192,512]{1,0:T(8,128)(2,1)} %get-tuple-element.85), channel_id=1, source_target_pairs={{0,24},{4,28},{8,16},{12,20},{16,8},{20,12},{24,0},{28,4},{1,25},{... | collective-permute-start | bytes 589832 | tf_op jit(solution)/shard_map/ppermute | solution.py:658
  111.1 24.4 %collective-permute-start.27 = (bf16[192,512]{1,0:T(8,128)(2,1)}, bf16[192,512]{1,0:T(8,128)(2,1)S(1)}, u32[]{:S(2)}, u32[]{:S(2)}) collective-permute-start(bf16[192,512]{1,0:T(8,128)(2,1)} %get-tuple-element.86), channel_id=1, source_target_pairs={{0,28},{4,24},{8,20},{12,16},{16,12},{20,8},{24,4},{28,0},{1,29},{... | collective-permute-start | bytes 589832 | tf_op jit(solution)/shard_map/ppermute | solution.py:658
  203.2 21.5 %collective-permute-start.43 = (bf16[192,512]{1,0:T(8,128)(2,1)}, bf16[192,512]{1,0:T(8,128)(2,1)S(1)}, u32[]{:S(2)}, u32[]{:S(2)}) collective-permute-start(bf16[192,512]{1,0:T(8,128)(2,1)} %get-tuple-element.94), channel_id=1, source_target_pairs={{0,8},{4,12},{8,0},{12,4},{16,24},{20,28},{24,16},{28,20},{1,9},{5... | collective-permute-start | bytes 589832 | tf_op jit(solution)/shard_map/ppermute | solution.py:658
  203.7 41.3 %collective-permute-start.44 = (bf16[192,512]{1,0:T(8,128)(2,1)}, bf16[192,512]{1,0:T(8,128)(2,1)S(1)}, u32[]{:S(2)}, u32[]{:S(2)}) collective-permute-start(bf16[192,512]{1,0:T(8,128)(2,1)} %get-tuple-element.95), channel_id=1, source_target_pairs={{0,12},{4,8},{8,4},{12,0},{16,28},{20,24},{24,20},{28,16},{1,13},{... | collective-permute-start | bytes 589832 | tf_op jit(solution)/shard_map/ppermute | solution.py:658
  206.0 39.1 %collective-permute-start.45 = (bf16[192,512]{1,0:T(8,128)(2,1)}, bf16[192,512]{1,0:T(8,128)(2,1)S(1)}, u32[]{:S(2)}, u32[]{:S(2)}) collective-permute-start(bf16[192,512]{1,0:T(8,128)(2,1)} %get-tuple-element.96), channel_id=1, source_target_pairs={{0,16},{4,20},{8,24},{12,28},{16,0},{20,4},{24,8},{28,12},{1,17},{... | collective-permute-start | bytes 589832 | tf_op jit(solution)/shard_map/ppermute | solution.py:658
  206.7 38.4 %collective-permute-start.46 = (bf16[192,512]{1,0:T(8,128)(2,1)}, bf16[192,512]{1,0:T(8,128)(2,1)S(1)}, u32[]{:S(2)}, u32[]{:S(2)}) collective-permute-start(bf16[192,512]{1,0:T(8,128)(2,1)} %get-tuple-element.97), channel_id=1, source_target_pairs={{0,20},{4,16},{8,28},{12,24},{16,4},{20,0},{24,12},{28,8},{1,21},{... | collective-permute-start | bytes 589832 | tf_op jit(solution)/shard_map/ppermute | solution.py:658
  222.5 22.6 %collective-permute-start.47 = (bf16[192,512]{1,0:T(8,128)(2,1)S(1)}, bf16[192,512]{1,0:T(8,128)(2,1)S(1)}, u32[]{:S(2)}, u32[]{:S(2)}) collective-permute-start(bf16[192,512]{1,0:T(8,128)(2,1)S(1)} %copy-done.43), channel_id=1, source_target_pairs={{0,24},{4,28},{8,16},{12,20},{16,8},{20,12},{24,0},{28,4},{1,25},{... | collective-permute-start | bytes 589832 | tf_op jit(solution)/shard_map/ppermute | solution.py:658
  290.0 24.8 %collective-permute-start.58 = (bf16[192,512]{1,0:T(8,128)(2,1)}, bf16[192,512]{1,0:T(8,128)(2,1)S(1)}, u32[]{:S(2)}, u32[]{:S(2)}) collective-permute-start(bf16[192,512]{1,0:T(8,128)(2,1)} %get-tuple-element.115), channel_id=1, source_target_pairs={{0,12},{4,8},{8,4},{12,0},{16,28},{20,24},{24,20},{28,16},{1,13},{... | collective-permute-start | bytes 589832 | tf_op jit(solution)/shard_map/ppermute | solution.py:658
  290.8 24.0 %collective-permute-start.59 = (bf16[192,512]{1,0:T(8,128)(2,1)}, bf16[192,512]{1,0:T(8,128)(2,1)S(1)}, u32[]{:S(2)}, u32[]{:S(2)}) collective-permute-start(bf16[192,512]{1,0:T(8,128)(2,1)} %get-tuple-element.116), channel_id=1, source_target_pairs={{0,16},{4,20},{8,24},{12,28},{16,0},{20,4},{24,8},{28,12},{1,17},{... | collective-permute-start | bytes 589832 | tf_op jit(solution)/shard_map/ppermute | solution.py:658
  292.8 22.0 %collective-permute-start.60 = (bf16[192,512]{1,0:T(8,128)(2,1)}, bf16[192,512]{1,0:T(8,128)(2,1)S(1)}, u32[]{:S(2)}, u32[]{:S(2)}) collective-permute-start(bf16[192,512]{1,0:T(8,128)(2,1)} %get-tuple-element.117), channel_id=1, source_target_pairs={{0,20},{4,16},{8,28},{12,24},{16,4},{20,0},{24,12},{28,8},{1,21},{... | collective-permute-start | bytes 589832 | tf_op jit(solution)/shard_map/ppermute | solution.py:658
  349.0 69.5 %collective-permute-start.94 = (bf16[1152,512]{1,0:T(8,128)(2,1)}, bf16[1152,512]{1,0:T(8,128)(2,1)}, u32[]{:S(2)}, u32[]{:S(2)}) collective-permute-start(bf16[1152,512]{1,0:T(8,128)(2,1)} %dynamic-slice_bitcast_fusion.1), channel_id=1, source_target_pairs={{0,1},{1,0},{2,3},{3,2},{4,5},{5,4},{6,7},{7,6},{8,9},{9,8},{10,11... | collective-permute-start | bytes 3538952 | tf_op jit(solution)/shard_map/ppermute | solution.py:594
  349.0 73.3 %collective-permute-start.106 = (bf16[1152,512]{1,0:T(8,128)(2,1)}, bf16[1152,512]{1,0:T(8,128)(2,1)}, u32[]{:S(2)}, u32[]{:S(2)}) collective-permute-start(bf16[1152,512]{1,0:T(8,128)(2,1)} %dynamic-slice_bitcast_fusion), channel_id=1, source_target_pairs={{0,1},{1,0},{2,3},{3,2},{4,5},{5,4},{6,7},{7,6},{8,9},{9,8},{10,11... | collective-permute-start | bytes 3538952 | tf_op jit(solution)/shard_map/ppermute | solution.py:594
  427.3 25.3 %collective-permute-start.95 = (bf16[576,512]{1,0:T(8,128)(2,1)}, bf16[576,512]{1,0:T(8,128)(2,1)}, u32[]{:S(2)}, u32[]{:S(2)}) collective-permute-start(bf16[576,512]{1,0:T(8,128)(2,1)} %dynamic-slice_bitcast_fusion.3), channel_id=1, source_target_pairs={{0,2},{1,3},{2,0},{3,1},{4,6},{5,7},{6,4},{7,5},{8,10},{9,11},{10,... | collective-permute-start | bytes 1769480 | tf_op jit(solution)/shard_map/ppermute | solution.py:594
  427.9 27.2 %collective-permute-start.107 = (bf16[576,512]{1,0:T(8,128)(2,1)S(1)}, bf16[576,512]{1,0:T(8,128)(2,1)}, u32[]{:S(2)}, u32[]{:S(2)}) collective-permute-start(bf16[576,512]{1,0:T(8,128)(2,1)S(1)} %dynamic-slice_bitcast_fusion.2), channel_id=1, source_target_pairs={{0,4},{1,5},{2,6},{3,7},{4,0},{5,1},{6,2},{7,3},{8,12},{9,13},{10,... | collective-permute-start | bytes 1769480 | tf_op jit(solution)/shard_map/ppermute | solution.py:594
  452.6 60.8 %collective-permute-start.93 = (bf16[512,512]{1,0:T(8,128)(2,1)}, bf16[512,512]{1,0:T(8,128)(2,1)}, u32[]{:S(2)}, u32[]{:S(2)}) collective-permute-start(bf16[512,512]{1,0:T(8,128)(2,1)} %bitcast.87), channel_id=1, source_target_pairs={{0,1},{1,0},{2,3},{3,2},{4,5},{5,4},{6,7},{7,6},{8,9},{9,8},{10,11... | collective-permute-start | bytes 1572872 | tf_op jit(solution)/shard_map/ppermute | solution.py:594
  (143 other events, 1214.7 us)
Sparse Core Ops, SparseCore 0:
  266.6 172.0 all-reduce.1
